TPU v7x, 256 devices: a whole 4x4x8 slice. The times are simulated.
256 devices in a mesh: pair: 64 (over x, z, core), fac: 4 (over y).
Axes of the slice: x: 4, y: 4, z: 8, core: 2. Of those that a mesh axis runs over, the one named last changes fastest.
Arguments:
- amplitudes: bfloat16 [256, 1024, 1024], P(('pair', 'fac')), may hold values from -6 to 6
- mirror_slot: int32 [256], P(('pair', 'fac')), may hold values from 0 to 0, as said below
- d_values: bfloat16 [4, 16, 64, 64], P('fac'), may hold values from -0.375 to 0.375
- d_cols: int32 [4, 16], P('fac'), may hold values from 0 to 15
- b_values: bfloat16 [4, 16, 64, 64], P('fac'), may hold values from -0.375 to 0.375
- b_cols: int32 [4, 16], P('fac'), may hold values from 0 to 15
Outputs:
- residual: bfloat16 [256, 1024, 1024], P(('pair', 'fac'))
Inputs may be any that keep to these rules, and one draw needn't show every extreme that they name: Mirrors are mutual: the pairs on device pair index p and fac index f have their mirrors on pair index (p + 64/2) mod 64 with the same fac index, and m(m(n)) = n; on each device mirror_slot is a permutation of its 1 slots.
All inputs are finite; a program needn't handle non-finite values.
Results may differ from a plain program's by a relative error of at most 0.0059.
Values may be sent and summed in bfloat16 or wider, within the bound.
A program may use at most 128 MiB of HBM per device.

v0:
```python
import jax
import jax.numpy as jnp
from jax import lax
from jax.sharding import PartitionSpec as P


def from_behind(shard, axis, by):
    count = lax.axis_size(axis)
    return lax.ppermute(shard, axis, [(i, (i + by) % count) for i in range(count)])


def pick_columns(columns, index):
    return jnp.take(columns, index, axis=2)


def dress_pairs(source, d_block, d_col, b_block, b_col):
    count = source.shape[0]
    size_v = source.shape[1]
    factors = d_col.shape[0]
    blocks = d_col.shape[1]
    width = size_v // blocks
    tiles = source.reshape(count, blocks, width, size_v)
    picked = jnp.take(tiles, d_col, axis=1)
    left = jnp.einsum("frab,pfrbv->pfrav", d_block, picked, preferred_element_type=jnp.bfloat16)
    columns = left.reshape(count, factors, size_v, blocks, width)
    chosen = jax.vmap(pick_columns, in_axes=(1, 0), out_axes=1)(columns, b_col)
    right = jnp.einsum("pfarb,frcb->parc", chosen, b_block, preferred_element_type=jnp.float32)
    return right.reshape(count, size_v, size_v)


def shards(amplitudes, mirror_slot, d_values, d_cols, b_values, b_cols):
    half = lax.axis_size("pair") // 2
    d_piece = lax.all_gather(d_values, "fac", axis=0, tiled=True)
    dcol_piece = lax.all_gather(d_cols, "fac", axis=0, tiled=True)
    b_piece = lax.all_gather(b_values, "fac", axis=0, tiled=True)
    bcol_piece = lax.all_gather(b_cols, "fac", axis=0, tiled=True)
    summed = dress_pairs(amplitudes, d_piece, dcol_piece, b_piece, bcol_piece)
    dressed = summed.astype(jnp.bfloat16)
    partner = from_behind(dressed, "pair", half)
    matched = jnp.take(partner, mirror_slot, axis=0)
    result = dressed.astype(jnp.float32) + jnp.swapaxes(matched, 1, 2).astype(jnp.float32)
    return result.astype(jnp.bfloat16)


def solution(mesh):
    placed = (
        P(("pair", "fac"), None, None),
        P(("pair", "fac")),
        P("fac", None, None, None),
        P("fac", None),
        P("fac", None, None, None),
        P("fac", None),
    )
    return jax.shard_map(
        shards,
        mesh=mesh,
        in_specs=placed,
        out_specs=P(("pair", "fac"), None, None),
        check_vma=False,
    )
```

profile of v0, /device:TPU:200, one launch (start us, length us, event | category | flops | bytes accessed | tf_op | source)
XLA Modules:
  0.0 161.6 jit_solution(5905376075243113790)
XLA Ops:
  0.0 0.0 copy-start
  0.0 8.2 %all-gather.1 = s32[4,1,16]{2,1,0:T(1,128)S(1)} all-gather(s32[1,1,16]{2,1,0:T(1,128)} %bitcast.47), channel_id=1, replica_groups=mesh['pair'=64,'fac'=4] {'fac'}, dimensions={0}, use_global_device_ids=true | all-gather | bytes 320 | tf_op jit(solution)/shard_map/all_gather | solution.py:34
  8.2 9.6 %all-gather = s32[4,1,16]{2,1,0:T(1,128)S(1)} all-gather(s32[1,1,16]{2,1,0:T(1,128)} %bitcast.48), channel_id=1, replica_groups=mesh['pair'=64,'fac'=4] {'fac'}, dimensions={0}, use_global_device_ids=true | all-gather | bytes 320 | tf_op jit(solution)/shard_map/all_gather | solution.py:36
  17.9 0.1 reshape.74
  18.0 14.2 %all_gather.14 = bf16[4,16,64,64]{3,2,1,0:T(8,128)(2,1)S(1)} all-gather(bf16[1,16,64,64]{3,2,1,0:T(8,128)(2,1)} %param.8), channel_id=1, replica_groups=mesh['pair'=64,'fac'=4] {'fac'}, dimensions={0}, use_global_device_ids=true | all-gather | bytes 655360 | tf_op jit(solution)/shard_map/all_gather | solution.py:33
  32.1 0.0 copy-done
  32.1 5.5 %gather_fusion = bf16[64,64,1024]{2,1,0:T(8,128)(2,1)} fusion(bf16[16,64,1024]{2,1,0:T(8,128)(2,1)S(1)} %bitcast.40, s32[1024]{0:T(1024)S(1)} %pad_clamp_fusion), kind=kCustom, calls=%fused_computation | custom fusion | bytes 16777472 | tf_op jit(solution)/shard_map/jit(_take)/gather | solution.py:23
  37.7 9.0 %fusion.7 = bf16[1,4,16,64,1024]{4,3,2,1,0:T(8,128)(2,1)} fusion(bf16[4,16,64,64]{3,2,1,0:T(8,128)(2,1)S(1)} %all_gather.14, bf16[4,16,64,1024]{3,2,1,0:T(8,128)(2,1)} %bitcast.42, pred[4,16]{1,0:T(4,128)(4,1)S(1)} %compare_and_fusion), kind=kOutput, calls=%fused_computation.9 | convolution fusion | flops 541065216 | bytes 17301568 | tf_op jit(solution)/shard_map/frab,pfrbv->pfrav/dot_general | solution.py:24
  46.7 22.1 %reshape.80 = bf16[4,1024,16,64]{3,2,1,0:T(8,128)(2,1)} reshape(bf16[1,4,16,64,1024]{4,3,2,1,0:T(8,128)(2,1)} %fusion.7) | data formatting | bytes 16777216 | tf_op jit(solution)/shard_map/vmap(jit(_take))/transpose | solution.py:13
  68.8 0.0 copy-start.2
  68.8 18.4 %copy.16 = bf16[4,1024,16,64]{1,3,2,0:T(8,128)(2,1)} copy(bf16[4,1024,16,64]{3,2,1,0:T(8,128)(2,1)} %reshape.80) | data formatting | bytes 16777216 | tf_op jit(solution)/shard_map/vmap(jit(_take))/transpose | solution.py:13
  87.1 0.1 reshape.82
  87.2 0.0 copy-done.2
  87.2 13.8 %all_gather.15 = bf16[4,16,64,64]{3,2,1,0:T(8,128)(2,1)S(1)} all-gather(bf16[1,16,64,64]{3,2,1,0:T(8,128)(2,1)S(1)} %copy-done.2), channel_id=1, replica_groups=mesh['pair'=64,'fac'=4] {'fac'}, dimensions={0}, use_global_device_ids=true | all-gather | bytes 655360 | tf_op jit(solution)/shard_map/all_gather | solution.py:35
  101.0 9.2 %gather_fusion.1 = bf16[64,1024,64]{1,2,0:T(8,128)(2,1)} fusion(bf16[4,1024,16,64]{1,3,2,0:T(8,128)(2,1)} %copy.16, s32[64]{0:T(128)S(1)} %reshape.82), kind=kCustom, calls=%fused_computation.1 | custom fusion | bytes 16777728 | tf_op jit(solution)/shard_map/vmap(jit(_take))/gather | solution.py:13
  110.3 6.8 %bitcast_convert_fusion = bf16[16,1024,64]{1,2,0:T(8,128)(2,1)} fusion(bf16[4,16,64,64]{3,2,1,0:T(8,128)(2,1)S(1)} %all_gather.15, bf16[4,16,1024,64]{2,3,1,0:T(8,128)(2,1)} %bitcast.41, pred[4,16]{1,0:T(4,128)(4,1)S(1)} %compare_and_fusion.1), kind=kOutput, calls=%fused_computation.12 | convolution fusion | flops 542113792 | bytes 11010112 | tf_op jit(solution)/shard_map/pfarb,frcb->parc/dot_general | solution.py:27
  117.1 3.0 %collective-permute-start = (bf16[1,1024,1024]{1,2,0:T(8,128)(2,1)}, bf16[1,1024,1024]{1,2,0:T(8,128)(2,1)}, u32[]{:S(2)}, u32[]{:S(2)}) collective-permute-start(bf16[1,1024,1024]{1,2,0:T(8,128)(2,1)} %bitcast.15), channel_id=1, source_target_pairs={{0,128},{4,132},{8,136},{12,140},{16,144},{20,148},{24,152},{28,15... | collective-permute-start | bytes 6291464 | tf_op jit(solution)/shard_map/ppermute | solution.py:9
  120.7 0.0 copy-start.1
  120.7 4.2 %bitcast_convert_fusion.1 = f32[1,1024,1024]{1,2,0:T(8,128)} fusion(bf16[1,1024,1024]{1,2,0:T(8,128)(2,1)} %bitcast.39), kind=kLoop, calls=%fused_computation.21 | loop fusion | flops 1048576 | bytes 6291456 | tf_op jit(solution)/shard_map/convert_element_type | solution.py:41
  124.9 5.4 %copy.17 = f32[1,1024,1024]{2,1,0:T(8,128)} copy(f32[1,1024,1024]{1,2,0:T(8,128)} %bitcast_convert_fusion.1) | data formatting | bytes 8388608 | tf_op jit(solution)/shard_map/convert_element_type | solution.py:41
  130.3 26.3 %collective-permute-done = bf16[1,1024,1024]{1,2,0:T(8,128)(2,1)} collective-permute-done((bf16[1,1024,1024]{1,2,0:T(8,128)(2,1)}, bf16[1,1024,1024]{1,2,0:T(8,128)(2,1)}, u32[]{:S(2)}, u32[]{:S(2)}) %collective-permute-start) | collective-permute-done | bytes 2097184 | tf_op jit(solution)/shard_map/ppermute | solution.py:9
  156.6 5.0 %fusion.10 = bf16[1,1024,1024]{2,1,0:T(8,128)(2,1)} fusion(f32[1,1024,1024]{2,1,0:T(8,128)} %copy.17, bf16[1,1024,1024]{1,2,0:T(8,128)(2,1)} %collective-permute-done, pred[]{:T(512)} %bitcast.16), kind=kLoop, calls=%fused_computation.11 | loop fusion | flops 4194304 | bytes 8388609 | tf_op jit(solution)/shard_map/convert_element_type | solution.py:42
  161.6 0.0 copy-done.1
  (5 shorter events, 0.0 us)
Async XLA Ops:
  0.0 32.1 %copy-start = (bf16[1,1024,1024]{2,1,0:T(8,128)(2,1)S(1)}, bf16[1,1024,1024]{2,1,0:T(8,128)(2,1)}, u32[]{:S(2)}) copy-start(bf16[1,1024,1024]{2,1,0:T(8,128)(2,1)} %param.6) | copy-start | bytes 6291460
  68.8 18.5 %copy-start.2 = (bf16[1,16,64,64]{3,2,1,0:T(8,128)(2,1)S(1)}, bf16[1,16,64,64]{3,2,1,0:T(8,128)(2,1)}, u32[]{:S(2)}) copy-start(bf16[1,16,64,64]{3,2,1,0:T(8,128)(2,1)} %param.10) | copy-start | bytes 393220
  117.1 39.6 %collective-permute-start = (bf16[1,1024,1024]{1,2,0:T(8,128)(2,1)}, bf16[1,1024,1024]{1,2,0:T(8,128)(2,1)}, u32[]{:S(2)}, u32[]{:S(2)}) collective-permute-start(bf16[1,1024,1024]{1,2,0:T(8,128)(2,1)} %bitcast.15), channel_id=1, source_target_pairs={{0,128},{4,132},{8,136},{12,140},{16,144},{20,148},{24,152},{28,15... | collective-permute-start | bytes 6291464 | tf_op jit(solution)/shard_map/ppermute | solution.py:9
  120.7 40.9 %copy-start.1 = (bf16[1,1024,1024]{2,1,0:T(8,128)(2,1)S(1)}, bf16[1,1024,1024]{2,1,0:T(8,128)(2,1)}, u32[]{:S(2)}) copy-start(bf16[1,1024,1024]{2,1,0:T(8,128)(2,1)} %param.6) | copy-start | bytes 6291460
where the time goes:
time: 163 us; the launch traced here: 162 us
  local copies, waits for them, and re-layouts  60.7 us (37%)
  blocking collectives  45.8 us (28%)
  waiting for transfers between devices  26.3 us (16%)
  matrix products  15.8 us (10%)
  other arithmetic  9.17 us (6%)
  starting transfers between devices  3.02 us (2%)
    transpose x2, local copies, waits for them, and re-layouts, pick_columns(): return jnp.take(columns, index, axis=2)  40.5 us
    ppermute x1, waiting for transfers between devices, from_behind(): lax.ppermute(shard, axis, [(i, (i + by) % count) for i in range(count)])  26.3 us
    all_gather x1, blocking collectives, shards(): d_piece = lax.all_gather(d_values, 'fac', axis=0, tiled=True)  14.2 us
    all_gather x1, blocking collectives, shards(): b_piece = lax.all_gather(b_values, 'fac', axis=0, tiled=True)  13.8 us
    all_gather x1, blocking collectives, shards(): bcol_piece = lax.all_gather(b_cols, 'fac', axis=0, tiled=True)  9.64 us
    gather x2, local copies, waits for them, and re-layouts, pick_columns(): return jnp.take(columns, index, axis=2)  9.3 us
    dot_general x1, matrix products, dress_pairs(): jnp.einsum('frab,pfrbv->pfrav', d_block, picked, preferred_element_type=j...  9 us
    all_gather x1, blocking collectives, shards(): dcol_piece = lax.all_gather(d_cols, 'fac', axis=0, tiled=True)  8.19 us
  transfers between devices with their start and end apart: 1, of which 1 were waited for; matrix products, arithmetic and copies ran while one was open for 6% of the time, Pallas kernels for 0%

commit v1 on v0

v1 whole, which is shorter than its diff:
```python
import jax
import jax.numpy as jnp
from jax import lax
from jax.experimental import pallas as pl
from jax.experimental.pallas import tpu as pltpu
from jax.sharding import PartitionSpec as P

MESH = pl.DeviceIdType.MESH
F32 = jnp.float32
BF16 = jnp.bfloat16
LANES = 128
GROUP = 256
NT = (((1,), (1,)), ((), ()))


def make_kernel(n_pair, n_fac, v, bs):
    nblk = v // bs
    chunks = v // LANES
    groups = v // GROUP
    per = GROUP // bs
    half = n_pair // 2

    def kernel(
        t_ref, slot_ref, d_ref, dcol_ref, b_ref, bcol_ref, out_ref,
        own_t, mirror_t, work_t, slot_s, d_land, b_land, dc_land, bc_land, dc_s, bc_s,
        d_diag, b_dense, left, left_k, acc, own_x,
        t_send, t_recv, f_send, f_recv, local_sem,
    ):
        p = lax.axis_index("pair")
        f = lax.axis_index("fac")
        mirror = (lax.rem(p + half, n_pair), f)

        def fac_peer(k):
            return (p, lax.rem(f + n_fac - k, n_fac))

        barrier = pltpu.get_barrier_semaphore()
        pl.semaphore_signal(barrier, inc=1, device_id=mirror, device_id_type=MESH)
        for k in range(1, n_fac):
            pl.semaphore_signal(barrier, inc=1, device_id=fac_peer(k), device_id_type=MESH)

        factors = ((d_ref, d_land), (dcol_ref, dc_land), (b_ref, b_land), (bcol_ref, bc_land))
        loads = [pltpu.make_async_copy(src, dst.at[0], local_sem.at[i]) for i, (src, dst) in enumerate(factors)]
        loads.append(pltpu.make_async_copy(t_ref, own_t, local_sem.at[4]))
        loads.append(pltpu.make_async_copy(slot_ref, slot_s, local_sem.at[5]))
        for load in loads:
            load.start()

        pl.semaphore_wait(barrier, n_fac)

        sends = []
        for k in range(1, n_fac):
            for i, (src, dst) in enumerate(factors):
                sends.append(pltpu.make_async_remote_copy(
                    src_ref=src, dst_ref=dst.at[k], send_sem=f_send.at[k, i], recv_sem=f_recv.at[k, i],
                    device_id=fac_peer(k), device_id_type=MESH))
        for j in range(chunks):
            sends.append(pltpu.make_async_remote_copy(
                src_ref=t_ref.at[:, :, pl.ds(j * LANES, LANES)], dst_ref=mirror_t.at[j],
                send_sem=t_send.at[j], recv_sem=t_recv.at[j], device_id=mirror, device_id_type=MESH))
        for send in sends:
            send.start()

        acc[...] = jnp.zeros_like(acc)
        rows_i = lax.broadcasted_iota(jnp.int32, (bs, LANES), 0)
        lanes_i = lax.broadcasted_iota(jnp.int32, (bs, LANES), 1)
        twice = jnp.where(lax.rem(lanes_i, bs) == rows_i, 1.0, 0.0).astype(BF16)
        which = lanes_i // bs

        for load in loads:
            load.wait()

        for k in range(n_fac):
            if k > 0:
                for send in sends[4 * (k - 1):4 * k]:
                    send.wait_recv()
            for i, (land, small) in enumerate(((dc_land, dc_s), (bc_land, bc_s))):
                move = pltpu.make_async_copy(land.at[k], small.at[k], local_sem.at[6 + i])
                move.start()
                move.wait()

            def build_d(g, _):
                rows = pl.ds(pl.multiple_of(g * GROUP, GROUP), GROUP)
                pair = jnp.dot(d_land[k, rows, :], twice, preferred_element_type=F32)
                for i in range(per):
                    part = pair[i * bs:(i + 1) * bs, :]
                    to = pl.ds(pl.multiple_of(g * GROUP + i * bs, bs), bs)
                    for h in range(GROUP // LANES):
                        piece = jnp.where(which + (LANES // bs) * h == i, part, 0.0)
                        d_diag[k, to, h * LANES:(h + 1) * LANES] = piece.astype(BF16)
                return 0

            lax.fori_loop(0, groups, build_d, 0)

            def build_b(c, _):
                rows = pl.ds(pl.multiple_of(c * bs, bs), bs)
                part = jnp.dot(b_land[k, rows, :], twice, preferred_element_type=F32)
                col = bc_s[k, 0, c]
                for j in range(chunks):
                    piece = jnp.where(which + (LANES // bs) * j == col, part, 0.0)
                    b_dense[j, rows, k * LANES:(k + 1) * LANES] = piece.astype(BF16)
                return 0

            lax.fori_loop(0, nblk, build_b, 0)

            def own_left(g, _):
                rows = pl.ds(pl.multiple_of(g * GROUP, GROUP), GROUP)
                picked = jnp.concatenate(
                    [own_t[dc_s[k, 0, g * per + i]] for i in range(per)], axis=0)
                left[rows, :] = jnp.dot(d_diag[k, rows, :], picked, preferred_element_type=F32).astype(BF16)
                return 0

            lax.fori_loop(0, groups, own_left, 0)

            def own_right(n, _):
                rows = pl.ds(pl.multiple_of(n * GROUP, GROUP), GROUP)
                right = jnp.concatenate([b_dense[j, rows, k * LANES:(k + 1) * LANES] for j in range(chunks)], axis=1)
                acc[:, rows] += lax.dot_general(left[...], right, NT, preferred_element_type=F32)
                return 0

            lax.fori_loop(0, groups, own_right, 0)

        own_x[...] = acc[...].astype(BF16)
        acc[...] = jnp.zeros_like(acc)
        base = slot_s[0] * nblk

        def mirror_left(j):
            work_t[...] = mirror_t[j]
            for k in range(n_fac):
                for g in range(groups):
                    rows = slice(g * GROUP, (g + 1) * GROUP)
                    picked = jnp.concatenate(
                        [work_t[base + dc_s[k, 0, g * per + i]] for i in range(per)], axis=0)
                    left_k[rows, k * LANES:(k + 1) * LANES] = jnp.dot(
                        d_diag[k, rows, :], picked, preferred_element_type=F32).astype(BF16)

        def mirror_step(j, _):
            pltpu.make_async_remote_copy(
                src_ref=t_ref.at[:, :, pl.ds(0, LANES)], dst_ref=mirror_t.at[j],
                send_sem=t_send.at[j], recv_sem=t_recv.at[j], device_id=mirror, device_id_type=MESH).wait_recv()
            mirror_left(j)
            acc[...] += lax.dot_general(b_dense[j], left_k[...], NT, preferred_element_type=F32)
            return 0

        lax.fori_loop(0, chunks - 1, mirror_step, 0)
        sends[-1].wait_recv()
        mirror_left(chunks - 1)
        other = acc[...] + lax.dot_general(b_dense[chunks - 1], left_k[...], NT, preferred_element_type=F32)
        out_ref[...] = (own_x[...].astype(F32) + other.astype(BF16).astype(F32)).astype(BF16)
        for send in sends:
            send.wait_send()

    return kernel


def shards(amplitudes, mirror_slot, d_values, d_cols, b_values, b_cols):
    n_pair, n_fac = lax.axis_size("pair"), lax.axis_size("fac")
    v = amplitudes.shape[1]
    bs = d_values.shape[-1]
    nblk = v // bs
    chunks = v // LANES
    anywhere = pl.BlockSpec(memory_space=pltpu.HBM)
    out = pl.pallas_call(
        make_kernel(n_pair, n_fac, v, bs),
        out_shape=pltpu.VMEM((v, v), BF16),
        in_specs=[anywhere] * 6,
        out_specs=pl.BlockSpec(memory_space=pltpu.VMEM),
        scratch_shapes=[
            pltpu.VMEM((nblk, bs, v), BF16),
            pltpu.VMEM((chunks, nblk, bs, LANES), BF16),
            pltpu.VMEM((nblk, bs, LANES), BF16),
            pltpu.SMEM((1,), jnp.int32),
            pltpu.VMEM((n_fac, v, bs), BF16),
            pltpu.VMEM((n_fac, v, bs), BF16),
            pltpu.VMEM((n_fac, 1, nblk), jnp.int32),
            pltpu.VMEM((n_fac, 1, nblk), jnp.int32),
            pltpu.SMEM((n_fac, 1, nblk), jnp.int32),
            pltpu.SMEM((n_fac, 1, nblk), jnp.int32),
            pltpu.VMEM((n_fac, v, GROUP), BF16),
            pltpu.VMEM((chunks, v, n_fac * LANES), BF16),
            pltpu.VMEM((v, v), BF16),
            pltpu.VMEM((v, n_fac * LANES), BF16),
            pltpu.VMEM((v, v), F32),
            pltpu.VMEM((v, v), BF16),
            pltpu.SemaphoreType.DMA((chunks,)),
            pltpu.SemaphoreType.DMA((chunks,)),
            pltpu.SemaphoreType.DMA((n_fac, 4)),
            pltpu.SemaphoreType.DMA((n_fac, 4)),
            pltpu.SemaphoreType.DMA((8,)),
        ],
        compiler_params=pltpu.CompilerParams(
            collective_id=0, has_side_effects=True, vmem_limit_bytes=56 * 2**20),
        name="ladder",
    )(
        amplitudes.reshape(nblk, bs, v), mirror_slot, d_values.reshape(v, bs), d_cols,
        b_values.reshape(v, bs), b_cols,
    )
    return out[None]


def solution(mesh):
    placed = (
        P(("pair", "fac"), None, None),
        P(("pair", "fac")),
        P("fac", None, None, None),
        P("fac", None),
        P("fac", None, None, None),
        P("fac", None),
    )
    return jax.shard_map(
        shards,
        mesh=mesh,
        in_specs=placed,
        out_specs=P(("pair", "fac"), None, None),
        check_vma=False,
    )
```

time: 163 us -> 63.3 us (0.39)
  Pallas kernels: 0 us -> 61.2 us
  local copies, waits for them, and re-layouts: 60.7 us -> 1.32 us
  blocking collectives: 45.8 us -> 0 us
  waiting for transfers between devices: 26.3 us -> 0 us
  matrix products: 15.8 us -> 0 us
  other arithmetic: 9.17 us -> 0 us
  starting transfers between devices: 3.02 us -> 0 us
    pallas_call x0 -> x1, Pallas kernels: none -> 61.2 us  [shards(): pl.pallas_call(make_kernel(n_pair, n_fac, v, bs), out_shape=pltpu.VMEM((v...]
    all_gather x4 -> x0, blocking collectives: 45.8 us -> none  [the longest x1 14.2 us: shards(): d_piece = lax.all_gather(d_values, 'fac', axis=0, tiled=True)]
    transpose x2 -> x0, local copies, waits for them, and re-layouts: 40.5 us -> none  [pick_columns(): return jnp.take(columns, index, axis=2)]
    ppermute x1 -> x0, waiting for transfers between devices: 26.3 us -> none  [from_behind(): lax.ppermute(shard, axis, [(i, (i + by) % count) for i in range(count)])]
    dot_general x2 -> x0, matrix products: 15.8 us -> none  [the longest x1 9 us: dress_pairs(): jnp.einsum('frab,pfrbv->pfrav', d_block, picked, preferred_element_type=j...]
    gather x3 -> x0, local copies, waits for them, and re-layouts: 14.8 us -> none  [the longest x2 9.3 us: pick_columns(): return jnp.take(columns, index, axis=2)]
    convert_element_type x2 -> x0, other arithmetic: 9.14 us -> none  [the longest x1 4.96 us: shards(): return result.astype(jnp.bfloat16)]
    convert_element_type x1 -> x0, local copies, waits for them, and re-layouts: 5.36 us -> none  [shards(): dressed.astype(jnp.float32)]
  transfers between devices with their start and end apart: 1 -> 0, of which waited for: 1 -> 0; matrix products, arithmetic and copies ran while one was open for 6% -> 0% of each run, Pallas kernels for 0% -> 0%
where the time goes in v1:
time: 63.3 us; the launch traced here: 63.2 us
  Pallas kernels  61.2 us (97%)
  local copies, waits for them, and re-layouts  1.32 us (2%)
  between operations  0.66 us (1%)
    pallas_call x1, Pallas kernels, shards(): pl.pallas_call(make_kernel(n_pair, n_fac, v, bs), out_shape=pltpu.VMEM((v...  61.2 us
    unnamed x1, local copies, waits for them, and re-layouts  1.32 us

profile of v1, /device:TPU:200, one launch (start us, length us, event | category | flops | bytes accessed | tf_op | source)
XLA Modules:
  0.0 63.2 jit_solution(3694879740792944448)
XLA Ops:
  0.7 61.2 %ladder.1 = bf16[1024,1024]{1,0:T(8,128)(2,1)S(1)} custom-call(bf16[16,64,1024]{2,1,0:T(8,128)(2,1)} %bitcast.5, s32[1]{0:T(128)S(6)} %copy.9.slot_ref, bf16[1024,64]{1,0:T(8,128)(2,1)} %bitcast.6, s32[1,16]{1,0:T(1,128)} %dcol_ref.1, bf16[1024,64]{1,0:T(8,128)(2,1)} %bitcast.7, s32[1,16]{1,0:T(1,128)} %bcol_ref.1), custom_call_target="tpu_custom_call" | custom-call | tf_op jit(solution)/shard_map/ladder/pallas_call | solution.py:162
  61.8 1.3 %copy.8 = bf16[1,1024,1024]{2,1,0:T(8,128)(2,1)} copy(bf16[1,1024,1024]{2,1,0:T(8,128)(2,1)S(1)} %bitcast.4) | data formatting | bytes 4194304

commit v2 on v1

v2 whole, which is shorter than its diff:
```python
import jax
import jax.numpy as jnp
from jax import lax
from jax.experimental import pallas as pl
from jax.experimental.pallas import tpu as pltpu
from jax.sharding import PartitionSpec as P

MESH = pl.DeviceIdType.MESH
F32 = jnp.float32
BF16 = jnp.bfloat16
LANES = 128
GROUP = 256
NT = (((1,), (1,)), ((), ()))


def make_kernel(n_pair, n_fac, v, bs):
    nblk = v // bs
    chunks = v // LANES
    groups = v // GROUP
    per = GROUP // bs
    half = n_pair // 2

    def kernel(
        t_ref, d_ref, dcol_ref, b_ref, bcol_ref, out_ref,
        own_t, mirror_t, work_t, d_in, b_in, land, dc_land, bc_land, dc_s, bc_s,
        d_diag, b_dense, left, left_k, acc, own_x,
        t_send, t_recv, f_send, f_recv, g_send, local_sem,
    ):
        p = lax.axis_index("pair")
        f = lax.axis_index("fac")
        mirror = (lax.rem(p + half, n_pair), f)

        def fac_peer(k):
            return (p, lax.rem(f + n_fac - k, n_fac))

        core = lax.rem(p, 2)
        sibling = (p + 1 - 2 * core, f)
        hub = core == 0

        barrier = pltpu.get_barrier_semaphore()
        pl.semaphore_signal(barrier, inc=1, device_id=mirror, device_id_type=MESH)

        @pl.when(hub)
        def _():
            for k in range(1, n_fac):
                pl.semaphore_signal(barrier, inc=1, device_id=fac_peer(k), device_id_type=MESH)

        @pl.when(core == 1)
        def _():
            pl.semaphore_signal(barrier, inc=1, device_id=sibling, device_id_type=MESH)

        pairs = ((d_ref, d_in), (b_ref, b_in), (dcol_ref, dc_land.at[0]), (bcol_ref, bc_land.at[0]),
                 (t_ref, own_t))
        loads = [pltpu.make_async_copy(src, dst, local_sem.at[i]) for i, (src, dst) in enumerate(pairs)]
        for load in loads:
            load.start()

        lower = lax.broadcasted_iota(jnp.int32, (bs, LANES), 1) - lax.broadcasted_iota(jnp.int32, (bs, LANES), 0)
        to_low = jnp.where(lower == 0, 1.0, 0.0).astype(BF16)
        to_high = jnp.where(lower == bs, 1.0, 0.0).astype(BF16)
        from_i = lax.broadcasted_iota(jnp.int32, (LANES, GROUP), 0)
        to_i = lax.broadcasted_iota(jnp.int32, (LANES, GROUP), 1)
        spread = jnp.where(to_i // LANES * bs + lax.rem(to_i, bs) == from_i, 1.0, 0.0).astype(BF16)
        which = lax.broadcasted_iota(jnp.int32, (16, LANES), 1) // bs
        mid = v // 2

        def mask(hit):
            return jnp.concatenate([jnp.where(hit, 1.0, 0.0).astype(BF16)] * (bs // 16), axis=0)

        for i, ref in enumerate((d_in, b_in)):
            loads[i].wait()
            low = jnp.dot(ref[0:mid, :], to_low, preferred_element_type=F32)
            high = jnp.dot(ref[mid:v, :], to_high, preferred_element_type=F32)
            land[0, i] = (low + high).astype(BF16)

        @pl.when(hub)
        def _():
            pl.semaphore_wait(barrier, n_fac + 1)

        @pl.when(core == 1)
        def _():
            pl.semaphore_wait(barrier, 1)

        t_sends = [
            pltpu.make_async_remote_copy(
                src_ref=t_ref.at[:, :, pl.ds(j * LANES, LANES)], dst_ref=mirror_t.at[j],
                send_sem=t_send.at[j], recv_sem=t_recv.at[j], device_id=mirror, device_id_type=MESH)
            for j in range(chunks)
        ]
        order = [1, n_fac - 1] + list(range(2, n_fac - 1))
        f_sends = {
            k: [
                pltpu.make_async_remote_copy(
                    src_ref=src, dst_ref=dst.at[k], send_sem=f_send.at[k, i], recv_sem=f_recv.at[k, i],
                    device_id=fac_peer(k), device_id_type=MESH)
                for i, (src, dst) in enumerate(((dcol_ref, dc_land), (bcol_ref, bc_land), (land.at[0], land)))
            ]
            for k in order
        }
        passes = {
            k: [
                pltpu.make_async_remote_copy(
                    src_ref=dst.at[k], dst_ref=dst.at[k], send_sem=g_send.at[k, i], recv_sem=f_recv.at[k, i],
                    device_id=sibling, device_id_type=MESH)
                for i, dst in enumerate((dc_land, bc_land, land))
            ]
            for k in order
        }

        t_sends[0].start()

        @pl.when(hub)
        def _():
            for k in order:
                for send in f_sends[k]:
                    send.start()

        for send in t_sends[1:]:
            send.start()

        def receive(k):
            for send in f_sends[k]:
                send.wait_recv()

            @pl.when(hub)
            def _():
                for send in passes[k]:
                    send.start()

        for load in loads[2:]:
            load.wait()

        for step, k in enumerate([0] + order):
            if step == 1:
                receive(order[0])
                receive(order[1])
            elif step == 2:
                for other in order[2:]:
                    receive(other)
            moves = [
                pltpu.make_async_copy(src.at[k], dst.at[k], local_sem.at[5 + i])
                for i, (src, dst) in enumerate(((dc_land, dc_s), (bc_land, bc_s)))
            ]
            for move in moves:
                move.start()

            twice = jnp.dot(land[k, 0], spread, preferred_element_type=F32).astype(BF16)
            none = jnp.zeros((bs, LANES), BF16)
            for r in range(nblk):
                h, i = divmod(r * bs, mid)
                part = twice[i:i + bs, h * LANES:(h + 1) * LANES]
                at = r % per * bs // LANES
                for side in range(GROUP // LANES):
                    piece = part * mask(which == r * bs % LANES // bs) if side == at else none
                    d_diag[k, r * bs:(r + 1) * bs, side * LANES:(side + 1) * LANES] = piece

            for move in moves:
                move.wait()
            twice = jnp.dot(land[k, 1], spread, preferred_element_type=F32).astype(BF16)
            for c in range(nblk):
                h, i = divmod(c * bs, mid)
                part = twice[i:i + bs, h * LANES:(h + 1) * LANES]
                col = bc_s[k, 0, c]
                for j in range(chunks):
                    piece = part * mask(which + (LANES // bs) * j == col)
                    b_dense[j, c * bs:(c + 1) * bs, k * LANES:(k + 1) * LANES] = piece

            for g in range(groups):
                rows = slice(g * GROUP, (g + 1) * GROUP)
                picked = jnp.concatenate([own_t[dc_s[k, 0, g * per + i]] for i in range(per)], axis=0)
                left[rows, :] = jnp.dot(d_diag[k, rows, :], picked, preferred_element_type=F32).astype(BF16)

            right = jnp.concatenate([b_dense[j, :, k * LANES:(k + 1) * LANES] for j in range(chunks)], axis=1)
            part = lax.dot_general(left[...], right, NT, preferred_element_type=F32)
            if step == 0:
                acc[...] = part
            elif step < n_fac - 1:
                acc[...] += part
            else:
                own_x[...] = (acc[...] + part).astype(BF16)

        def mirror_part(j):
            work_t[...] = mirror_t[j]
            for k in range(n_fac):
                for g in range(groups):
                    rows = slice(g * GROUP, (g + 1) * GROUP)
                    picked = jnp.concatenate([work_t[dc_s[k, 0, g * per + i]] for i in range(per)], axis=0)
                    left_k[rows, k * LANES:(k + 1) * LANES] = jnp.dot(
                        d_diag[k, rows, :], picked, preferred_element_type=F32).astype(BF16)
            return lax.dot_general(b_dense[j], left_k[...], NT, preferred_element_type=F32)

        t_sends[0].wait_recv()
        acc[...] = mirror_part(0)

        def mirror_step(j, _):
            pltpu.make_async_remote_copy(
                src_ref=t_ref.at[:, :, pl.ds(0, LANES)], dst_ref=mirror_t.at[j],
                send_sem=t_send.at[j], recv_sem=t_recv.at[j], device_id=mirror, device_id_type=MESH).wait_recv()
            acc[...] += mirror_part(j)
            return 0

        lax.fori_loop(1, chunks - 1, mirror_step, 0)
        t_sends[-1].wait_recv()
        other = (acc[...] + mirror_part(chunks - 1)).astype(BF16)
        out_ref[...] = (own_x[...].astype(F32) + other.astype(F32)).astype(BF16)
        for send in t_sends:
            send.wait_send()

        @pl.when(hub)
        def _():
            for k in order:
                for send in f_sends[k] + passes[k]:
                    send.wait_send()

    return kernel


def shards(amplitudes, mirror_slot, d_values, d_cols, b_values, b_cols):
    n_pair, n_fac = lax.axis_size("pair"), lax.axis_size("fac")
    v = amplitudes.shape[1]
    bs = d_values.shape[-1]
    nblk = v // bs
    chunks = v // LANES
    anywhere = pl.BlockSpec(memory_space=pltpu.HBM)
    out = pl.pallas_call(
        make_kernel(n_pair, n_fac, v, bs),
        out_shape=pltpu.VMEM((v, v), BF16),
        in_specs=[anywhere] * 5,
        out_specs=pl.BlockSpec(memory_space=pltpu.VMEM),
        scratch_shapes=[
            pltpu.VMEM((nblk, bs, v), BF16),
            pltpu.VMEM((chunks, nblk, bs, LANES), BF16),
            pltpu.VMEM((nblk, bs, LANES), BF16),
            pltpu.VMEM((v, bs), BF16),
            pltpu.VMEM((v, bs), BF16),
            pltpu.VMEM((n_fac, 2, v // 2, LANES), BF16),
            pltpu.VMEM((n_fac, 1, nblk), jnp.int32),
            pltpu.VMEM((n_fac, 1, nblk), jnp.int32),
            pltpu.SMEM((n_fac, 1, nblk), jnp.int32),
            pltpu.SMEM((n_fac, 1, nblk), jnp.int32),
            pltpu.VMEM((n_fac, v, GROUP), BF16),
            pltpu.VMEM((chunks, v, n_fac * LANES), BF16),
            pltpu.VMEM((v, v), BF16),
            pltpu.VMEM((v, n_fac * LANES), BF16),
            pltpu.VMEM((v, v), F32),
            pltpu.VMEM((v, v), BF16),
            pltpu.SemaphoreType.DMA((chunks,)),
            pltpu.SemaphoreType.DMA((chunks,)),
            pltpu.SemaphoreType.DMA((n_fac, 3)),
            pltpu.SemaphoreType.DMA((n_fac, 3)),
            pltpu.SemaphoreType.DMA((n_fac, 3)),
            pltpu.SemaphoreType.DMA((7,)),
        ],
        compiler_params=pltpu.CompilerParams(
            collective_id=0, has_side_effects=True, vmem_limit_bytes=56 * 2**20),
        name="ladder",
    )(
        amplitudes.reshape(nblk, bs, v), d_values.reshape(v, bs), d_cols,
        b_values.reshape(v, bs), b_cols,
    )
    return jnp.take(out[None], mirror_slot, axis=0, mode="clip")


def solution(mesh):
    placed = (
        P(("pair", "fac"), None, None),
        P(("pair", "fac")),
        P("fac", None, None, None),
        P("fac", None),
        P("fac", None, None, None),
        P("fac", None),
    )
    return jax.shard_map(
        shards,
        mesh=mesh,
        in_specs=placed,
        out_specs=P(("pair", "fac"), None, None),
        check_vma=False,
    )
```

time: 63.3 us -> 54.2 us (0.86)
  Pallas kernels: 61.2 us -> 52.8 us
  between operations: 0.66 us -> 0.01 us
    pallas_call x1, Pallas kernels: 61.2 us -> 52.8 us  [shards(): pl.pallas_call(make_kernel(n_pair, n_fac, v, bs), out_shape=pltpu.VMEM((v...]
where the time goes in v2:
time: 54.2 us; the launch traced here: 54.1 us
  Pallas kernels  52.8 us (97%)
  local copies, waits for them, and re-layouts  1.32 us (2%)
    pallas_call x1, Pallas kernels, shards(): pl.pallas_call(make_kernel(n_pair, n_fac, v, bs), out_shape=pltpu.VMEM((v...  52.8 us
    unnamed x1, local copies, waits for them, and re-layouts  1.32 us

profile of v2, /device:TPU:200, one launch (start us, length us, event | category | flops | bytes accessed | tf_op | source)
XLA Modules:
  0.0 54.1 jit_solution(17843349524080995511)
XLA Ops:
  0.0 52.8 %ladder.1 = bf16[1024,1024]{1,0:T(8,128)(2,1)S(1)} custom-call(bf16[16,64,1024]{2,1,0:T(8,128)(2,1)} %bitcast.5, bf16[1024,64]{1,0:T(8,128)(2,1)} %bitcast.6, s32[1,16]{1,0:T(1,128)} %dcol_ref.1, bf16[1024,64]{1,0:T(8,128)(2,1)} %bitcast.7, s32[1,16]{1,0:T(1,128)} %bcol_ref.1), custom_call_target="tpu_custom_call" | custom-call | tf_op jit(solution)/shard_map/ladder/pallas_call | solution.py:225
  52.8 1.3 %copy.8 = bf16[1,1024,1024]{2,1,0:T(8,128)(2,1)} copy(bf16[1,1024,1024]{2,1,0:T(8,128)(2,1)S(1)} %bitcast.4) | data formatting | bytes 4194304

commit v3 on v2

--- a/solution.py
+++ b/solution.py
@@ -21,9 +21,9 @@
     half = n_pair // 2
 
     def kernel(
-        t_ref, d_ref, dcol_ref, b_ref, bcol_ref, out_ref,
-        own_t, mirror_t, work_t, d_in, b_in, land, dc_land, bc_land, dc_s, bc_s,
-        d_diag, b_dense, left, left_k, acc, own_x,
+        t_ref, d_ref, dcol_ref, b_ref, bcol_ref, acc, left_k, b_last,
+        own_t, mirror_t, work_t, last_t, d_in, b_in, land, dc_land, bc_land, dc_s, bc_s,
+        d_diag, b_dense, left,
         t_send, t_recv, f_send, f_recv, g_send, local_sem,
     ):
         p = lax.axis_index("pair")
@@ -67,12 +67,6 @@
         def mask(hit):
             return jnp.concatenate([jnp.where(hit, 1.0, 0.0).astype(BF16)] * (bs // 16), axis=0)
 
-        for i, ref in enumerate((d_in, b_in)):
-            loads[i].wait()
-            low = jnp.dot(ref[0:mid, :], to_low, preferred_element_type=F32)
-            high = jnp.dot(ref[mid:v, :], to_high, preferred_element_type=F32)
-            land[0, i] = (low + high).astype(BF16)
-
         @pl.when(hub)
         def _():
             pl.semaphore_wait(barrier, n_fac + 1)
@@ -83,7 +77,7 @@
 
         t_sends = [
             pltpu.make_async_remote_copy(
-                src_ref=t_ref.at[:, :, pl.ds(j * LANES, LANES)], dst_ref=mirror_t.at[j],
+                src_ref=t_ref.at[:, :, pl.ds(j * LANES, LANES)], dst_ref=mirror_t.at[j] if j < chunks - 1 else last_t,
                 send_sem=t_send.at[j], recv_sem=t_recv.at[j], device_id=mirror, device_id_type=MESH)
             for j in range(chunks)
         ]
@@ -107,16 +101,20 @@
             for k in order
         }
 
-        t_sends[0].start()
+        for send in t_sends:
+            send.start()
 
         @pl.when(hub)
         def _():
             for k in order:
-                for send in f_sends[k]:
+                for send in f_sends[k][:2]:
                     send.start()
 
-        for send in t_sends[1:]:
-            send.start()
+        for i, ref in enumerate((d_in, b_in)):
+            loads[i].wait()
+            low = jnp.dot(ref[0:mid, :], to_low, preferred_element_type=F32)
+            high = jnp.dot(ref[mid:v, :], to_high, preferred_element_type=F32)
+            land[0, i] = (low + high).astype(BF16)
 
         def receive(k):
             for send in f_sends[k]:
@@ -154,6 +152,12 @@
                     piece = part * mask(which == r * bs % LANES // bs) if side == at else none
                     d_diag[k, r * bs:(r + 1) * bs, side * LANES:(side + 1) * LANES] = piece
 
+            if step == 0:
+                @pl.when(hub)
+                def _():
+                    for other in order:
+                        f_sends[other][2].start()
+
             for move in moves:
                 move.wait()
             twice = jnp.dot(land[k, 1], spread, preferred_element_type=F32).astype(BF16)
@@ -163,46 +167,45 @@
                 col = bc_s[k, 0, c]
                 for j in range(chunks):
                     piece = part * mask(which + (LANES // bs) * j == col)
-                    b_dense[j, c * bs:(c + 1) * bs, k * LANES:(k + 1) * LANES] = piece
+                    (b_dense.at[j] if j < chunks - 1 else b_last)[c * bs:(c + 1) * bs, k * LANES:(k + 1) * LANES] = piece
 
             for g in range(groups):
                 rows = slice(g * GROUP, (g + 1) * GROUP)
                 picked = jnp.concatenate([own_t[dc_s[k, 0, g * per + i]] for i in range(per)], axis=0)
                 left[rows, :] = jnp.dot(d_diag[k, rows, :], picked, preferred_element_type=F32).astype(BF16)
 
-            right = jnp.concatenate([b_dense[j, :, k * LANES:(k + 1) * LANES] for j in range(chunks)], axis=1)
+            right = jnp.concatenate(
+                [b_dense[j, :, k * LANES:(k + 1) * LANES] for j in range(chunks - 1)]
+                + [b_last[:, k * LANES:(k + 1) * LANES]], axis=1)
             part = lax.dot_general(left[...], right, NT, preferred_element_type=F32)
             if step == 0:
                 acc[...] = part
             elif step < n_fac - 1:
                 acc[...] += part
             else:
-                own_x[...] = (acc[...] + part).astype(BF16)
-
-        def mirror_part(j):
-            work_t[...] = mirror_t[j]
+                acc[...] = (acc[...] + part).astype(BF16).astype(F32)
+
+        def mirror_left(source):
             for k in range(n_fac):
                 for g in range(groups):
                     rows = slice(g * GROUP, (g + 1) * GROUP)
-                    picked = jnp.concatenate([work_t[dc_s[k, 0, g * per + i]] for i in range(per)], axis=0)
+                    picked = jnp.concatenate([source[dc_s[k, 0, g * per + i]] for i in range(per)], axis=0)
                     left_k[rows, k * LANES:(k + 1) * LANES] = jnp.dot(
                         d_diag[k, rows, :], picked, preferred_element_type=F32).astype(BF16)
-            return lax.dot_general(b_dense[j], left_k[...], NT, preferred_element_type=F32)
-
-        t_sends[0].wait_recv()
-        acc[...] = mirror_part(0)
+
 
         def mirror_step(j, _):
             pltpu.make_async_remote_copy(
                 src_ref=t_ref.at[:, :, pl.ds(0, LANES)], dst_ref=mirror_t.at[j],
                 send_sem=t_send.at[j], recv_sem=t_recv.at[j], device_id=mirror, device_id_type=MESH).wait_recv()
-            acc[...] += mirror_part(j)
+            work_t[...] = mirror_t[j]
+            mirror_left(work_t)
+            acc[...] += lax.dot_general(b_dense[j], left_k[...], NT, preferred_element_type=F32)
             return 0
 
-        lax.fori_loop(1, chunks - 1, mirror_step, 0)
+        lax.fori_loop(0, chunks - 1, mirror_step, 0)
         t_sends[-1].wait_recv()
-        other = (acc[...] + mirror_part(chunks - 1)).astype(BF16)
-        out_ref[...] = (own_x[...].astype(F32) + other.astype(F32)).astype(BF16)
+        mirror_left(last_t)
         for send in t_sends:
             send.wait_send()
 
@@ -213,6 +216,22 @@
                     send.wait_send()
 
     return kernel
+
+
+def finish(acc, left_k, b_last, out_ref, stage, sem):
+    v = acc.shape[1]
+    half = v // 2
+    blocks = [(0, half, 0), (half, half, 0), (0, half, half), (half, half // 2, half), (v - half // 2, half // 2, half)]
+    copies = []
+    for i, (m, rows, n) in enumerate(blocks):
+        at = (slice(m, m + rows), slice(n, n + half))
+        part = lax.dot_general(b_last[at[0], :], left_k[at[1], :], NT, preferred_element_type=F32)
+        stage[at] = (acc[at] + part).astype(BF16)
+        copy = pltpu.make_async_copy(stage.at[at], out_ref.at[at], sem.at[i])
+        copy.start()
+        copies.append(copy)
+    for copy in copies:
+        copy.wait()
 
 
 def shards(amplitudes, mirror_slot, d_values, d_cols, b_values, b_cols):
@@ -222,14 +241,19 @@
     nblk = v // bs
     chunks = v // LANES
     anywhere = pl.BlockSpec(memory_space=pltpu.HBM)
-    out = pl.pallas_call(
+    parts = pl.pallas_call(
         make_kernel(n_pair, n_fac, v, bs),
-        out_shape=pltpu.VMEM((v, v), BF16),
+        out_shape=(
+            pltpu.VMEM((v, v), F32),
+            pltpu.VMEM((v, n_fac * LANES), BF16),
+            pltpu.VMEM((v, n_fac * LANES), BF16),
+        ),
         in_specs=[anywhere] * 5,
-        out_specs=pl.BlockSpec(memory_space=pltpu.VMEM),
+        out_specs=[pl.BlockSpec(memory_space=pltpu.VMEM)] * 3,
         scratch_shapes=[
             pltpu.VMEM((nblk, bs, v), BF16),
-            pltpu.VMEM((chunks, nblk, bs, LANES), BF16),
+            pltpu.VMEM((chunks - 1, nblk, bs, LANES), BF16),
+            pltpu.VMEM((nblk, bs, LANES), BF16),
             pltpu.VMEM((nblk, bs, LANES), BF16),
             pltpu.VMEM((v, bs), BF16),
             pltpu.VMEM((v, bs), BF16),
@@ -239,10 +263,7 @@
             pltpu.SMEM((n_fac, 1, nblk), jnp.int32),
             pltpu.SMEM((n_fac, 1, nblk), jnp.int32),
             pltpu.VMEM((n_fac, v, GROUP), BF16),
-            pltpu.VMEM((chunks, v, n_fac * LANES), BF16),
-            pltpu.VMEM((v, v), BF16),
-            pltpu.VMEM((v, n_fac * LANES), BF16),
-            pltpu.VMEM((v, v), F32),
+            pltpu.VMEM((chunks - 1, v, n_fac * LANES), BF16),
             pltpu.VMEM((v, v), BF16),
             pltpu.SemaphoreType.DMA((chunks,)),
             pltpu.SemaphoreType.DMA((chunks,)),
@@ -252,12 +273,21 @@
             pltpu.SemaphoreType.DMA((7,)),
         ],
         compiler_params=pltpu.CompilerParams(
-            collective_id=0, has_side_effects=True, vmem_limit_bytes=56 * 2**20),
+            collective_id=0, has_side_effects=True, vmem_limit_bytes=40 * 2**20),
         name="ladder",
-    )(
-        amplitudes.reshape(nblk, bs, v), d_values.reshape(v, bs), d_cols,
-        b_values.reshape(v, bs), b_cols,
-    )
+    )(*(
+        pltpu.with_memory_space_constraint(x, pltpu.HBM)
+        for x in (amplitudes.reshape(nblk, bs, v), d_values.reshape(v, bs), d_cols, b_values.reshape(v, bs), b_cols)
+    ))
+    out = pl.pallas_call(
+        finish,
+        out_shape=jax.ShapeDtypeStruct((v, v), BF16),
+        in_specs=[pl.BlockSpec(memory_space=pltpu.VMEM)] * 3,
+        out_specs=pl.BlockSpec(memory_space=pl.ANY),
+        scratch_shapes=[pltpu.VMEM((v, v), BF16), pltpu.SemaphoreType.DMA((5,))],
+        compiler_params=pltpu.CompilerParams(vmem_limit_bytes=40 * 2**20),
+        name="finish",
+    )(*parts)
     return jnp.take(out[None], mirror_slot, axis=0, mode="clip")
 
 

time: 54.2 us -> 52.7 us (0.972)
  local copies, waits for them, and re-layouts: 1.32 us -> 0 us
    unnamed x1 -> x0, local copies, waits for them, and re-layouts: 1.32 us -> none
    pallas_call x1 -> x2, Pallas kernels: 52.8 us -> 52.4 us  [the longest x1 50.4 us: shards(): pl.pallas_call(make_kernel(n_pair, n_fac, v, bs), out_shape=(pltpu.VMEM((...]
where the time goes in v3:
time: 52.7 us; the launch traced here: 52.6 us
  Pallas kernels  52.4 us (99%)
    pallas_call x1, Pallas kernels, shards(): pl.pallas_call(make_kernel(n_pair, n_fac, v, bs), out_shape=(pltpu.VMEM((...  50.4 us
    pallas_call x1, Pallas kernels, shards(): pl.pallas_call(finish, out_shape=jax.ShapeDtypeStruct((v, v), BF16), in_s...  2.04 us

profile of v3, /device:TPU:200, one launch (start us, length us, event | category | flops | bytes accessed | tf_op | source)
XLA Modules:
  0.0 52.6 jit_solution(1997471557048786528)
XLA Ops:
  0.0 50.4 %ladder.1 = (f32[1024,1024]{1,0:T(8,128)S(1)}, bf16[1024,512]{1,0:T(8,128)(2,1)S(1)}, bf16[1024,512]{1,0:T(8,128)(2,1)S(1)}) custom-call(bf16[16,64,1024]{2,1,0:T(8,128)(2,1)} %bitcast.4, bf16[1024,64]{1,0:T(8,128)(2,1)} %bitcast.5, s32[1,16]{1,0:T(1,128)} %dcol_ref.1, bf16[1024,64]{1,0:T(8,128)(2,1)} %bitcast.6, s32[1,16]{1,0:T(1,128)} %bcol_ref.1), custom_call_target="tpu_custom_call" | custom-call | tf_op jit(solution)/shard_map/ladder/pallas_call | solution.py:244
  50.4 2.0 %finish.1 = bf16[1024,1024]{1,0:T(8,128)(2,1)} custom-call(f32[1024,1024]{1,0:T(8,128)S(1)} %get-tuple-element.8.acc, bf16[1024,512]{1,0:T(8,128)(2,1)S(1)} %get-tuple-element.9.left_k, bf16[1024,512]{1,0:T(8,128)(2,1)S(1)} %get-tuple-element.10.b_last), custom_call_target="tpu_custom_call" | custom-call | tf_op jit(solution)/shard_map/finish/pallas_call | solution.py:282

commit v4 on v3

--- a/solution.py
+++ b/solution.py
@@ -101,8 +101,12 @@
             for k in order
         }
 
-        for send in t_sends:
+        for send in t_sends[:-1]:
             send.start()
+
+        @pl.when(hub)
+        def _():
+            t_sends[-1].start()
 
         @pl.when(hub)
         def _():
@@ -198,6 +202,11 @@
             pltpu.make_async_remote_copy(
                 src_ref=t_ref.at[:, :, pl.ds(0, LANES)], dst_ref=mirror_t.at[j],
                 send_sem=t_send.at[j], recv_sem=t_recv.at[j], device_id=mirror, device_id_type=MESH).wait_recv()
+
+            @pl.when(jnp.logical_and(core == 1, j == chunks - 2))
+            def _():
+                t_sends[-1].start()
+
             work_t[...] = mirror_t[j]
             mirror_left(work_t)
             acc[...] += lax.dot_general(b_dense[j], left_k[...], NT, preferred_element_type=F32)

time: 52.7 us -> 53.5 us (1.015)
  the two profiles are of different devices: /device:TPU:200 before, /device:TPU:1 now
where the time goes in v4:
time: 53.5 us; the launch traced here: 53.4 us
  Pallas kernels  53.3 us (100%)
    pallas_call x1, Pallas kernels, shards(): pl.pallas_call(make_kernel(n_pair, n_fac, v, bs), out_shape=(pltpu.VMEM((...  51.2 us
    pallas_call x1, Pallas kernels, shards(): pl.pallas_call(finish, out_shape=jax.ShapeDtypeStruct((v, v), BF16), in_s...  2.04 us

profile of v4, /device:TPU:1, one launch (start us, length us, event | category | flops | bytes accessed | tf_op | source)
XLA Modules:
  0.0 53.4 jit_solution(17289511249072461390)
XLA Ops:
  0.0 51.2 %ladder.1 = (f32[1024,1024]{1,0:T(8,128)S(1)}, bf16[1024,512]{1,0:T(8,128)(2,1)S(1)}, bf16[1024,512]{1,0:T(8,128)(2,1)S(1)}) custom-call(bf16[16,64,1024]{2,1,0:T(8,128)(2,1)} %bitcast.4, bf16[1024,64]{1,0:T(8,128)(2,1)} %bitcast.5, s32[1,16]{1,0:T(1,128)} %dcol_ref.1, bf16[1024,64]{1,0:T(8,128)(2,1)} %bitcast.6, s32[1,16]{1,0:T(1,128)} %bcol_ref.1), custom_call_target="tpu_custom_call" | custom-call | tf_op jit(solution)/shard_map/ladder/pallas_call | solution.py:253
  51.2 2.0 %finish.1 = bf16[1024,1024]{1,0:T(8,128)(2,1)} custom-call(f32[1024,1024]{1,0:T(8,128)S(1)} %get-tuple-element.8.acc, bf16[1024,512]{1,0:T(8,128)(2,1)S(1)} %get-tuple-element.9.left_k, bf16[1024,512]{1,0:T(8,128)(2,1)S(1)} %get-tuple-element.10.b_last), custom_call_target="tpu_custom_call" | custom-call | tf_op jit(solution)/shard_map/finish/pallas_call | solution.py:291

commit v5 on v4

--- a/solution.py
+++ b/solution.py
@@ -199,14 +199,14 @@
 
 
         def mirror_step(j, _):
+            @pl.when(jnp.logical_and(core == 1, j == chunks - 2))
+            def _():
+                t_sends[-2].wait_send()
+                t_sends[-1].start()
+
             pltpu.make_async_remote_copy(
                 src_ref=t_ref.at[:, :, pl.ds(0, LANES)], dst_ref=mirror_t.at[j],
                 send_sem=t_send.at[j], recv_sem=t_recv.at[j], device_id=mirror, device_id_type=MESH).wait_recv()
-
-            @pl.when(jnp.logical_and(core == 1, j == chunks - 2))
-            def _():
-                t_sends[-1].start()
-
             work_t[...] = mirror_t[j]
             mirror_left(work_t)
             acc[...] += lax.dot_general(b_dense[j], left_k[...], NT, preferred_element_type=F32)
@@ -215,11 +215,12 @@
         lax.fori_loop(0, chunks - 1, mirror_step, 0)
         t_sends[-1].wait_recv()
         mirror_left(last_t)
-        for send in t_sends:
+        for send in t_sends[:-2] + t_sends[-1:]:
             send.wait_send()
 
         @pl.when(hub)
         def _():
+            t_sends[-2].wait_send()
             for k in order:
                 for send in f_sends[k] + passes[k]:
                     send.wait_send()

time: 53.5 us -> 52.9 us (0.989)
  the two profiles are of different devices: /device:TPU:1 before, /device:TPU:200 now
where the time goes in v5:
time: 52.9 us; the launch traced here: 52.6 us
  Pallas kernels  52.4 us (99%)
    pallas_call x1, Pallas kernels, shards(): pl.pallas_call(make_kernel(n_pair, n_fac, v, bs), out_shape=(pltpu.VMEM((...  50.4 us
    pallas_call x1, Pallas kernels, shards(): pl.pallas_call(finish, out_shape=jax.ShapeDtypeStruct((v, v), BF16), in_s...  2.04 us

profile of v5, /device:TPU:200, one launch (start us, length us, event | category | flops | bytes accessed | tf_op | source)
XLA Modules:
  0.0 52.6 jit_solution(5557429888188932637)
XLA Ops:
  0.0 50.4 %ladder.1 = (f32[1024,1024]{1,0:T(8,128)S(1)}, bf16[1024,512]{1,0:T(8,128)(2,1)S(1)}, bf16[1024,512]{1,0:T(8,128)(2,1)S(1)}) custom-call(bf16[16,64,1024]{2,1,0:T(8,128)(2,1)} %bitcast.4, bf16[1024,64]{1,0:T(8,128)(2,1)} %bitcast.5, s32[1,16]{1,0:T(1,128)} %dcol_ref.1, bf16[1024,64]{1,0:T(8,128)(2,1)} %bitcast.6, s32[1,16]{1,0:T(1,128)} %bcol_ref.1), custom_call_target="tpu_custom_call" | custom-call | tf_op jit(solution)/shard_map/ladder/pallas_call | solution.py:254
  50.4 2.0 %finish.1 = bf16[1024,1024]{1,0:T(8,128)(2,1)} custom-call(f32[1024,1024]{1,0:T(8,128)S(1)} %get-tuple-element.8.acc, bf16[1024,512]{1,0:T(8,128)(2,1)S(1)} %get-tuple-element.9.left_k, bf16[1024,512]{1,0:T(8,128)(2,1)S(1)} %get-tuple-element.10.b_last), custom_call_target="tpu_custom_call" | custom-call | tf_op jit(solution)/shard_map/finish/pallas_call | solution.py:292
